TPU v7x, 256 devices: a whole 4x4x8 slice. The times are simulated.
256 devices in a mesh: row: 8 (over y, core), col: 32 (over x, z).
Axes of the slice: x: 4, y: 4, z: 8, core: 2. Of those that a mesh axis runs over, the one named last changes fastest.
Arguments:
- kkt: float32 [8192, 8192], P('row', 'col'), may hold values from -4 to 4, as said below
- swaps: int32 [2, 2, 128], replicated, may hold values from 0 to 8191, as said below
- inverses: float32 [2, 256, 256], replicated
- pivots: float32 [2, 256], replicated, may hold values from -0.12 to 0.12
- couplings: float32 [2, 256], replicated, may hold values from -0.12 to 0.12
- pattern: int32 [2, 256], replicated, may hold values from 0 to 1, as said below
Outputs:
- factored: float32 [8192, 8192], P('row', 'col')
Inputs may be any that keep to these rules, and one draw needn't show every extreme that they name: For panel k, swaps[k, 0, :] holds 128 distinct rows among k * 256 to k * 256 + 255, both ends of that range among them, and swaps[k, 1, :] holds 128 distinct rows among (k + 1) * 256 to 8191, both ends of that range among them. pattern[k, i] = 1 makes rows i and i + 1 one 2 x 2 block of D; no two neighbouring entries are both 1 and the last entry is 0. kkt is the stored order of a symmetric matrix.
All inputs are finite; a program needn't handle non-finite values.
Results may differ from a plain program's by a relative error of at most 0.00014.
Values sent between devices are 32-bit elements; how exact they have to be, the bound alone decides.
A program may use at most 64 MiB of HBM per device.

v0:
```python
import jax
import jax.numpy as jnp
from jax import lax
from jax.sharding import Mesh
from jax.sharding import PartitionSpec as P

COL = ("col_0", "col_1")
HI = lax.Precision.HIGHEST


def tdot(a, b):
    return lax.dot_general(
        a, b, (((0,), (0,)), ((), ())), precision=HI, preferred_element_type=jnp.float32
    )


def swapped(rows, lead, partner):
    to_partner = rows[:, None] == lead[None, :]
    to_lead = rows[:, None] == partner[None, :]
    moved = jnp.sum(
        jnp.where(to_partner, partner[None, :], 0) + jnp.where(to_lead, lead[None, :], 0), axis=1
    )
    return jnp.where(jnp.any(to_partner | to_lead, axis=1), moved, rows)


def plan(swaps, tile, row_groups, dtype=jnp.float32):
    width = tile // row_groups
    count = swaps.shape[2]
    partner = swaps[:, 1, :].reshape(-1)
    top = jnp.arange(2 * tile, dtype=jnp.int32)
    rows = jnp.concatenate([top, partner])
    source = swapped(swapped(rows, swaps[1, 0], swaps[1, 1]), swaps[0, 0], swaps[0, 1])
    repeated = jnp.any(swaps[0, 1][:, None] == swaps[1, 1][None, :], axis=1)
    valid = jnp.concatenate([~repeated, jnp.ones((count,), bool)]) & (partner >= 2 * tile)
    sliced = source.reshape(3, row_groups, width).transpose(1, 0, 2)
    return (rows, source, sliced, jnp.where(valid, partner, -1))


def hits(rows, first, tile):
    return (rows[:, None] == first + jnp.arange(tile, dtype=jnp.int32)[None, :]).astype(jnp.float32)


def along_d(lower_t, pivot, coupling, pattern):
    links = coupling * pattern.astype(jnp.float32)
    zero = jnp.zeros((1, lower_t.shape[1]), lower_t.dtype)
    after = jnp.concatenate([lower_t[1:], zero], axis=0)
    before = jnp.concatenate([zero, lower_t[:-1]], axis=0)
    links_before = jnp.concatenate([jnp.zeros((1,), links.dtype), links[:-1]])
    return lower_t * pivot[:, None] + after * links[:, None] + before * links_before[:, None]


def exchange(picked, moves, tile, row_groups, x_size):
    width = tile // row_groups
    row_index = lax.axis_index("row")
    z_index = lax.axis_index("col_1")
    piece = lax.psum_scatter(picked, "row", scatter_dimension=0, tiled=False)
    strip = lax.all_gather(piece, "row")
    mine = lax.psum(jnp.where(z_index == row_index, strip, 0.0), "col_1")
    wide = lax.all_gather(mine, "col_0")
    part = jnp.dot(piece, moves, precision=HI, preferred_element_type=jnp.float32)
    t0, t1, tp = (part[:width], part[width : 2 * width], part[2 * width :])
    corner = jnp.stack(
        [
            t0[:, 2 * tile :],
            t1[:, 2 * tile :],
            tp[:, 2 * tile :],
            t0[:, tile : 2 * tile],
            t0[:, :tile],
            t1[:, tile : 2 * tile],
        ]
    )
    corner = lax.all_gather(lax.psum(corner, COL), "row")
    return (strip, wide, corner)


def shards(kkt, swaps, inverses, pivots, couplings, pattern):
    tile = inverses.shape[1]
    row_groups = lax.axis_size("row")
    x_size = lax.axis_size("col_0")
    z_size = lax.axis_size("col_1")
    row_index = lax.axis_index("row")
    col_index = lax.axis_index(COL)
    rows, source, sliced, partner = plan(swaps, tile, row_groups)
    flat = sliced.reshape(-1)
    owned = flat // tile % row_groups == row_index
    taken = jnp.take(kkt, flat // tile // row_groups * tile + flat % tile, axis=0)
    picked = jnp.where(owned[:, None], taken, 0.0).reshape(row_groups, -1, tile)
    moves = hits(source, col_index * tile, tile).T
    strip, wide, corner = exchange(picked, moves, tile, row_groups, x_size)

    def ordered(piece):
        return piece.reshape(row_groups, 3, -1, tile).transpose(1, 0, 2, 3).reshape(-1, tile)

    corner = corner.transpose(1, 0, 2, 3).reshape(6, tile, tile)
    to_partner = corner[0:3].reshape(3 * tile, tile)
    block_01, block_00, block_11 = (corner[3], corner[4], corner[5])
    tiles = [row_index + row_groups * slot for slot in range(x_size)] + [col_index]
    strips = [ordered(wide[slot]) for slot in range(x_size)] + [ordered(strip)]
    marks = [hits(partner, index * tile, tile) for index in tiles]
    keep = [1.0 - jnp.sum(mark, axis=0) for mark in marks]
    fixed = [
        strips[n] * keep[n][None, :]
        + jnp.dot(to_partner, marks[n], precision=HI, preferred_element_type=jnp.float32)
        for n in range(x_size + 1)
    ]
    upper = [jnp.where(tiles[n] == 1, block_01, fixed[n][:tile]) for n in range(x_size + 1)]
    low0 = [jnp.where(tiles[n] > 0, tdot(inverses[0], upper[n]), 0.0) for n in range(x_size + 1)]
    low0_1 = tdot(inverses[0], block_01)
    scaled0_1 = along_d(low0_1, pivots[0], couplings[0], pattern[0])
    scaled0 = along_d(low0[-1], pivots[0], couplings[0], pattern[0])
    low1 = [
        jnp.where(
            tiles[n] > 1,
            tdot(inverses[1], fixed[n][tile : 2 * tile] - tdot(scaled0_1, low0[n])),
            0.0,
        )
        for n in range(x_size + 1)
    ]
    scaled1 = along_d(low1[-1], pivots[1], couplings[1], pattern[1])
    outs = []
    for n in range(x_size):
        base = kkt[n * tile : (n + 1) * tile] * keep[n][:, None] * keep[-1][None, :]
        base = base + tdot(marks[n], fixed[-1][2 * tile :])
        base = base + tdot(fixed[n][2 * tile :] * keep[n][None, :], marks[-1])
        value = base - tdot(low0[n], scaled0) - tdot(low1[n], scaled1)
        value = jnp.where(tiles[n] == 0, scaled0, value)
        value = jnp.where(tiles[n] == 1, scaled1, value)
        at_0 = jnp.where(tiles[n] == 0, block_00, low0[n].T)
        at_1 = jnp.where(tiles[n] == 0, scaled0_1, low1[n].T)
        at_1 = jnp.where(tiles[n] == 1, block_11 - tdot(low0_1, scaled0_1), at_1)
        value = jnp.where(col_index == 0, at_0, value)
        value = jnp.where(col_index == 1, at_1, value)
        outs.append(value)
    return jnp.concatenate(outs, axis=0)


def solution(mesh):
    z_size = mesh.shape["row"]
    finer = Mesh(mesh.devices.reshape(mesh.shape["row"], -1, z_size), ("row", "col_0", "col_1"))
    in_specs = (P("row", COL), P(), P(), P(), P(), P())
    return jax.shard_map(
        shards, mesh=finer, in_specs=in_specs, out_specs=P("row", COL), check_vma=False
    )
```

profile of v0, /device:TPU:1, one launch (start us, length us, event | category | flops | bytes accessed | tf_op | source)
XLA Modules:
  0.0 369.6 jit_solution(7685777161819229525)
XLA Ops:
  6.5 0.8 slice_bitcast_fusion.9
  7.3 0.7 slice.199
  9.6 3.3 gather_fusion
  12.9 1.2 select_select_fusion
  14.2 35.9 %reduce-scatter.2.cloned.1.call-done = f32[1,96,256]{2,1,0:T(8,128)} async-done(((f32[8,96,256]{2,1,0:T(8,128)}), f32[1,96,256]{2,1,0:T(8,128)}) %reduce-scatter.2.cloned.1.call-update) | async-done | bytes 98320 | tf_op jit(solution)/shard_map/reduce_scatter | solution.py:56
  50.1 1.5 fusion.17
  51.6 0.7 copy-done.4
  52.4 16.4 %all_gather.17 = f32[8,96,256]{2,1,0:T(8,128)S(1)} all-gather(f32[1,96,256]{2,1,0:T(8,128)} %reduce-scatter.2.cloned.1.call-done), channel_id=1, replica_groups=mesh['row'=8,'col_0'=4,'col_1'=8] {'row'}, dimensions={0}, use_global_device_ids=true | all-gather | bytes 884736 | tf_op jit(solution)/shard_map/all_gather | solution.py:57
  68.8 1.0 select_bitcast_fusion
  69.8 124.7 %all-reduce.10.cloned.1.call-done = f32[1,6,32,256]{3,2,1,0:T(8,128)} async-done(((f32[1,6,32,256]{3,2,1,0:T(8,128)}), f32[1,6,32,256]{3,2,1,0:T(8,128)}) %all-reduce.10.cloned.1.call-update) | async-done | bytes 196624 | tf_op jit(solution)/shard_map/psum | solution.py:72
  195.3 73.7 %all-reduce.12.cloned.1.call-done = f32[1,8,96,256]{3,2,1,0:T(8,128)} async-done(((f32[1,8,96,256]{3,2,1,0:T(8,128)}), f32[1,8,96,256]{3,2,1,0:T(8,128)}) %all-reduce.12.cloned.1.call-update) | async-done | bytes 786448 | tf_op jit(solution)/shard_map/psum | solution.py:58
  269.2 31.6 %all-gather.3.cloned.1.call-done = f32[8,6,32,256]{3,2,1,0:T(8,128)} async-done(((f32[1,6,32,256]{3,2,1,0:T(8,128)}), f32[8,6,32,256]{3,2,1,0:T(8,128)}) %all-gather.3.cloned.1.call-update) | async-done | bytes 1572880 | tf_op jit(solution)/shard_map/all_gather | solution.py:72
  300.8 1.5 copy.51
  302.4 0.8 fusion.125
  304.6 0.6 convolution_select_fusion.7
  306.1 0.6 fusion.8
  307.3 1.2 convolution_add_fusion.6
  310.6 33.6 %all-gather.5.cloned.1.call-done = f32[4,8,96,256]{3,2,1,0:T(8,128)} async-done(((f32[1,8,96,256]{3,2,1,0:T(8,128)}), f32[4,8,96,256]{3,2,1,0:T(8,128)}) %all-gather.5.cloned.1.call-update) | async-done | bytes 3145744 | tf_op jit(solution)/shard_map/all_gather | solution.py:59
  344.2 2.2 fusion.124
  350.0 0.6 convolution_select_fusion.1
  352.3 0.8 convolution_subtract_fusion.5
  354.3 0.6 convolution_select_fusion.5
  356.4 0.6 bitcast_select_fusion.3
  362.1 1.0 pad_maximum_fusion
  (107 shorter events, 20.4 us)
Async XLA Ops:
  6.5 43.5 %reduce-scatter.2.cloned.1.call-start = ((), (), s32[]{:S(2)}) async-start(), calls=%async_computation.1 | async-start | bytes 884736 | tf_op jit(solution)/shard_map/reduce_scatter | solution.py:56
  14.1 180.4 %all-reduce.10.cloned.1.call-start = ((), (), s32[]{:S(2)}) async-start(), calls=%async_computation.2 | async-start | bytes 393216 | tf_op jit(solution)/shard_map/psum | solution.py:72
  51.6 0.7 copy-start.4
  52.3 142.9 %copy-start.5 = (s32[2,256]{1,0:T(2,128)S(1)}, s32[2,256]{1,0:T(2,128)}, u32[]{:S(2)}) copy-start(s32[2,256]{1,0:T(2,128)} %param.11) | copy-start | bytes 6148
  52.3 142.9 %copy-start.6 = (f32[2,256]{1,0:T(2,128)S(1)}, f32[2,256]{1,0:T(2,128)}, u32[]{:S(2)}) copy-start(f32[2,256]{1,0:T(2,128)} %param.10) | copy-start | bytes 6148
  52.4 216.6 %all-reduce.12.cloned.1.call-start = ((), (), s32[]{:S(2)}) async-start(), calls=%async_computation.4 | async-start | bytes 1572864 | tf_op jit(solution)/shard_map/psum | solution.py:58
  68.8 200.2 %copy-start.7 = (f32[2,256]{1,0:T(2,128)S(1)}, f32[2,256]{1,0:T(2,128)}, u32[]{:S(2)}) copy-start(f32[2,256]{1,0:T(2,128)} %param.9) | copy-start | bytes 6148
  69.8 231.1 %all-gather.3.cloned.1.call-start = ((), (), s32[]{:S(2)}) async-start(), calls=%async_computation.3 | async-start | bytes 1769472 | tf_op jit(solution)/shard_map/all_gather | solution.py:72
  194.5 149.6 %all-gather.5.cloned.1.call-start = ((), (), s32[]{:S(2)}) async-start(), calls=%async_computation.5 | async-start | bytes 3932160 | tf_op jit(solution)/shard_map/all_gather | solution.py:59
  302.4 1.0 copy-start.1
  306.1 1.2 copy-start
  348.6 1.0 copy-start.2
  354.9 1.5 copy-start.3
Sparse Core Ops, SparseCore 0:
  14.2 35.8 reduce-scatter.1
  53.5 140.9 all-reduce.9
  196.8 72.0 all-reduce.11
  270.6 30.1 all-gather.2
  302.5 41.6 all-gather.4
where the time goes:
time: 370 us
  waiting for transfers between devices  300 us (81%)
  matrix products  22.2 us (6%)
  blocking collectives  16.4 us (4%)
  between operations  13.9 us (4%)
  local copies, waits for them, and re-layouts  11.6 us (3%)
  other arithmetic  5.64 us (2%)
    psum x1, waiting for transfers between devices, exchange(): corner = lax.all_gather(lax.psum(corner, COL), 'row')  125 us
    psum x1, waiting for transfers between devices, exchange(): mine = lax.psum(jnp.where(z_index == row_index, strip, 0.0), 'col_1')  73.7 us
    reduce_scatter x1, waiting for transfers between devices, exchange(): piece = lax.psum_scatter(picked, 'row', scatter_dimension=0, tiled=False)  35.9 us
    all_gather x1, waiting for transfers between devices, exchange(): wide = lax.all_gather(mine, 'col_0')  33.6 us
    all_gather x1, waiting for transfers between devices, exchange(): corner = lax.all_gather(lax.psum(corner, COL), 'row')  31.6 us
    dot_general x33, matrix products, tdot(): lax.dot_general(a, b, (((0,), (0,)), ((), ())), precision=HI, preferred_e...  17.9 us
    all_gather x1, blocking collectives, exchange(): strip = lax.all_gather(piece, 'row')  16.4 us
  transfers between devices with their start and end apart: 5, of which 5 were waited for; matrix products, arithmetic and copies ran while one was open for 3% of the time, Pallas kernels for 0%

commit v1 on v0

--- a/solution.py
+++ b/solution.py
@@ -69,7 +69,7 @@
             t1[:, tile : 2 * tile],
         ]
     )
-    corner = lax.all_gather(lax.psum(corner, COL), "row")
+    corner = lax.all_gather(lax.psum(lax.psum(corner, "col_0"), "col_1"), "row")
     return (strip, wide, corner)
 
 

time: 370 us -> 276 us (0.75)
  waiting for transfers between devices: 300 us -> 205 us
    psum x2, waiting for transfers between devices: 198 us -> 105 us  [exchange(): corner = lax.all_gather(lax.psum(lax.psum(corner, 'col_0'), 'col_1'), 'row')]
  transfers between devices with their start and end apart: 5 -> 5, of which waited for: 5 -> 5; matrix products, arithmetic and copies ran while one was open for 3% -> 4% of each run, Pallas kernels for 0% -> 0%
where the time goes in v1:
time: 276 us; the launch traced here: 275 us
  waiting for transfers between devices  205 us (74%)
  matrix products  22.2 us (8%)
  blocking collectives  16.4 us (6%)
  between operations  13.9 us (5%)
  local copies, waits for them, and re-layouts  11.6 us (4%)
  other arithmetic  5.64 us (2%)
    psum x2, waiting for transfers between devices, exchange(): corner = lax.all_gather(lax.psum(lax.psum(corner, 'col_0'), 'col_1'), 'row')  105 us
    reduce_scatter x1, waiting for transfers between devices, exchange(): piece = lax.psum_scatter(picked, 'row', scatter_dimension=0, tiled=False)  35.9 us
    all_gather x1, waiting for transfers between devices, exchange(): wide = lax.all_gather(mine, 'col_0')  33.6 us
    all_gather x1, waiting for transfers between devices, exchange(): corner = lax.all_gather(lax.psum(lax.psum(corner, 'col_0'), 'col_1'), 'row')  30.8 us
    dot_general x33, matrix products, tdot(): lax.dot_general(a, b, (((0,), (0,)), ((), ())), precision=HI, preferred_e...  17.9 us
    all_gather x1, blocking collectives, exchange(): strip = lax.all_gather(piece, 'row')  16.4 us
  transfers between devices with their start and end apart: 5, of which 5 were waited for; matrix products, arithmetic and copies ran while one was open for 4% of the time, Pallas kernels for 0%

profile of v1, /device:TPU:1, one launch (start us, length us, event | category | flops | bytes accessed | tf_op | source)
XLA Modules:
  0.0 275.2 jit_solution(16788505355199296939)
XLA Ops:
  6.5 0.8 slice_bitcast_fusion.9
  7.3 0.7 slice.199
  9.6 3.3 %gather_fusion = f32[768,256]{1,0:T(8,128)S(1)} fusion(f32[1024,256]{1,0:T(8,128)} %param.6, s32[1024]{0:T(1024)S(1)} %pad_clamp_fusion), kind=kCustom, calls=%fused_computation | custom fusion | bytes 1575936 | tf_op jit(solution)/shard_map/jit(_take)/gather | solution.py:86
  12.9 1.2 select_select_fusion
  14.2 35.9 %reduce-scatter.2.cloned.1.call-done = f32[1,96,256]{2,1,0:T(8,128)} async-done(((f32[8,96,256]{2,1,0:T(8,128)}), f32[1,96,256]{2,1,0:T(8,128)}) %reduce-scatter.2.cloned.1.call-update) | async-done | bytes 98320 | tf_op jit(solution)/shard_map/reduce_scatter | solution.py:56
  50.1 1.5 fusion.17
  51.6 0.7 copy-done.4
  52.4 16.4 %all_gather.17 = f32[8,96,256]{2,1,0:T(8,128)S(1)} all-gather(f32[1,96,256]{2,1,0:T(8,128)} %reduce-scatter.2.cloned.1.call-done), channel_id=1, replica_groups=mesh['row'=8,'col_0'=4,'col_1'=8] {'row'}, dimensions={0}, use_global_device_ids=true | all-gather | bytes 884736 | tf_op jit(solution)/shard_map/all_gather | solution.py:57
  68.8 1.0 select_bitcast_fusion
  69.7 28.5 %all-reduce.11.cloned.1.call-done = f32[6,32,256]{2,1,0:T(8,128)} async-done(((f32[6,32,256]{2,1,0:T(8,128)}), f32[6,32,256]{2,1,0:T(8,128)}) %all-reduce.11.cloned.1.call-update) | async-done | bytes 196624 | tf_op jit(solution)/shard_map/psum | solution.py:72
  98.3 76.3 %all-reduce.13.cloned.1.call-done = (f32[1,6,32,256]{3,2,1,0:T(8,128)}, f32[1,8,96,256]{3,2,1,0:T(8,128)}) async-done(((f32[1,6,32,256]{3,2,1,0:T(8,128)}, f32[1,8,96,256]{3,2,1,0:T(8,128)}), (f32[1,6,32,256]{3,2,1,0:T(8,128)}, f32[1,8,96,256]{3,2,1,0:T(8,128)})) %all-reduce.13.cloned.1.call-update) | async-done | bytes 983056 | tf_op jit(solution)/shard_map/psum | solution.py:72
  175.6 30.8 %all-gather.3.cloned.1.call-done = f32[8,6,32,256]{3,2,1,0:T(8,128)} async-done(((f32[1,6,32,256]{3,2,1,0:T(8,128)}), f32[8,6,32,256]{3,2,1,0:T(8,128)}) %all-gather.3.cloned.1.call-update) | async-done | bytes 1572880 | tf_op jit(solution)/shard_map/all_gather | solution.py:72
  206.4 1.5 copy.51
  208.0 0.8 fusion.125
  210.1 0.6 convolution_select_fusion.7
  211.0 0.6 convolution_subtract_fusion.11
  211.6 0.6 fusion.8
  212.9 1.2 convolution_add_fusion.6
  216.1 33.6 %all-gather.5.cloned.1.call-done = f32[4,8,96,256]{3,2,1,0:T(8,128)} async-done(((f32[1,8,96,256]{3,2,1,0:T(8,128)}), f32[4,8,96,256]{3,2,1,0:T(8,128)}) %all-gather.5.cloned.1.call-update) | async-done | bytes 3145744 | tf_op jit(solution)/shard_map/all_gather | solution.py:59
  249.7 2.2 fusion.124
  257.2 0.6 convolution_select_fusion.3
  257.8 0.8 convolution_subtract_fusion.5
  262.0 0.6 bitcast_select_fusion.3
  267.6 1.0 pad_maximum_fusion
  (107 shorter events, 20.4 us)
Async XLA Ops:
  6.5 43.5 %reduce-scatter.2.cloned.1.call-start = ((), (), s32[]{:S(2)}) async-start(), calls=%async_computation.1 | async-start | bytes 884736 | tf_op jit(solution)/shard_map/reduce_scatter | solution.py:56
  14.1 84.1 %all-reduce.11.cloned.1.call-start = ((), (), s32[]{:S(2)}) async-start(), calls=%async_computation.2 | async-start | bytes 393216 | tf_op jit(solution)/shard_map/psum | solution.py:72
  51.6 0.7 copy-start.4
  52.3 122.2 %all-reduce.13.cloned.1.call-start = ((), (), s32[]{:S(2)}) async-start(), calls=%async_computation.5 | async-start | bytes 1966080 | tf_op jit(solution)/shard_map/psum | solution.py:72
  68.8 106.5 %copy-start.5 = (s32[2,256]{1,0:T(2,128)S(1)}, s32[2,256]{1,0:T(2,128)}, u32[]{:S(2)}) copy-start(s32[2,256]{1,0:T(2,128)} %param.11) | copy-start | bytes 6148
  68.8 106.5 %copy-start.6 = (f32[2,256]{1,0:T(2,128)S(1)}, f32[2,256]{1,0:T(2,128)}, u32[]{:S(2)}) copy-start(f32[2,256]{1,0:T(2,128)} %param.10) | copy-start | bytes 6148
  68.8 106.7 %copy-start.7 = (f32[2,256]{1,0:T(2,128)S(1)}, f32[2,256]{1,0:T(2,128)}, u32[]{:S(2)}) copy-start(f32[2,256]{1,0:T(2,128)} %param.9) | copy-start | bytes 6148
  98.2 108.1 %all-gather.3.cloned.1.call-start = ((), (), s32[]{:S(2)}) async-start(), calls=%async_computation.3 | async-start | bytes 1769472 | tf_op jit(solution)/shard_map/all_gather | solution.py:72
  174.6 75.1 %all-gather.5.cloned.1.call-start = ((), (), s32[]{:S(2)}) async-start(), calls=%async_computation.4 | async-start | bytes 3932160 | tf_op jit(solution)/shard_map/all_gather | solution.py:59
  207.9 1.0 copy-start.1
  211.6 1.2 copy-start
  254.2 1.0 copy-start.2
  260.5 1.5 copy-start.3
Sparse Core Ops, SparseCore 0:
  14.2 35.8 reduce-scatter.1
  52.5 45.7 all-reduce.10
  100.7 73.8 all-reduce.12
  176.3 30.0 all-gather.2
  208.0 41.6 all-gather.4
